TPU v7x, 32 devices: a whole 2x2x4 slice. The times are simulated.
32 devices in a mesh: dp: 16 (over z, y, core), mp: 2 (over x).
Axes of the slice: x: 2, y: 2, z: 4, core: 2. Of those that a mesh axis runs over, the one named last changes fastest.
Arguments:
- activations: bfloat16 [8192, 28672], P('dp', 'mp'), may hold values from -200 to 200
- weight: bfloat16 [8192, 28672], P(None, ('mp', 'dp')), may hold values from -25 to 25
- thresholds: float32 [8192], P('dp'), may hold values from 0.5 to 1.5
Outputs:
- pruned: bfloat16 [8192, 28672], P('dp', 'mp')
All inputs are finite; a program needn't handle non-finite values.
Results may differ from a plain program's by a relative error of at most 0.0004.
Values may be sent and summed in bfloat16 or wider, within the bound.
No kernel may reach another device: no remote copies, remote signals or barrier semaphores. Data moves between devices by JAX's collectives and lax.ppermute only.
A program may use at most 128 MiB of HBM per device.

v0:
```python
import jax
import jax.numpy as jnp
from jax import lax
from jax.sharding import PartitionSpec as P

IN = 28672
gate_slope = 2.0
small_eps = 1e-06


def soft_prune(block, col_norm, row_total, limit):
    wide = block.astype(jnp.float32)
    scores = jnp.abs(wide) * col_norm[None, :]
    row_mean = row_total[:, None] / IN + small_eps
    kept_share = jnp.clip((scores / row_mean - limit[:, None]) * gate_slope + 0.5, 0.0, 1.0)
    return (wide * kept_share).astype(jnp.bfloat16)


def per_device(activations, weight, thresholds):
    partial_value = jnp.sum(jnp.square(activations.astype(jnp.float32)), axis=0)
    relaid = lax.all_to_all(weight, "dp", split_axis=0, concat_axis=1, tiled=True)
    squares = lax.psum(partial_value, "dp")
    col_norm = jnp.sqrt(squares)
    row_part = jnp.sum(jnp.abs(relaid.astype(jnp.float32)) * col_norm[None, :], axis=1)
    row_total = lax.psum(row_part, "mp")
    return soft_prune(relaid, col_norm, row_total, thresholds)


def solution(mesh):
    placed = (P("dp", "mp"), P(None, ("mp", "dp")), P("dp"))
    return jax.shard_map(
        per_device, mesh=mesh, in_specs=placed, out_specs=P("dp", "mp"), check_vma=False
    )
```

profile of v0, /device:TPU:0, one launch (start us, length us, event | category | flops | bytes accessed | tf_op | source)
XLA Modules:
  0.0 432.1 jit_solution(9146727415281544940)
XLA Ops:
  0.0 7.5 %all-to-all-start = ((bf16[16,512,896]{2,1,0:T(8,128)(2,1)}), bf16[16,512,896]{2,1,0:T(8,128)(2,1)}, u32[]{:S(2)}, u32[]{:S(2)}) async-start(bf16[16,512,896]{2,1,0:T(8,128)(2,1)} %bitcast.22), calls=%async_computation | async-start | bytes 29360128 | tf_op jit(solution)/shard_map/all_to_all | solution.py:21
  7.5 8.5 %multiply_reduce_fusion = f32[14336]{0:T(1024)S(1)} fusion(bf16[512,14336]{1,0:T(8,128)(2,1)} %param.3), kind=kLoop, calls=%fused_computation.12 | loop fusion | flops 22005760 | bytes 14737408 | tf_op jit(solution)/shard_map/reduce_sum | solution.py:20
  16.0 347.7 %psum.14 = f32[14336]{0:T(1024)S(1)} all-reduce(f32[14336]{0:T(1024)S(1)} %multiply_reduce_fusion), channel_id=1, replica_groups=mesh['dp'=16,'mp'=2] {'dp'}, use_global_device_ids=true, to_apply=%region_1.0 | all-reduce | flops 14336 | bytes 114688 | tf_op jit(solution)/shard_map/psum | solution.py:22
  363.7 0.0 all-to-all-done
  363.7 20.7 %copy.5 = bf16[16,512,896]{1,2,0:T(8,128)(2,1)} copy(bf16[16,512,896]{2,1,0:T(8,128)(2,1)} %all-to-all-done) | data formatting | bytes 29360128 | tf_op jit(solution)/shard_map/all_to_all | solution.py:21
  384.4 0.0 copy-start
  384.4 6.9 %fusion.1 = f32[512]{0:T(512)S(1)} fusion(bf16[16,512,896]{1,2,0:T(8,128)(2,1)} %copy.5, f32[16,896]{1,0:T(8,128)S(1)} %mul.31), kind=kLoop, calls=%fused_computation.4 | loop fusion | flops 29359616 | bytes 14739456 | tf_op jit(solution)/shard_map/reduce_sum | solution.py:24
  391.3 4.9 %psum.15 = f32[512]{0:T(512)S(1)} all-reduce(f32[512]{0:T(512)S(1)} %fusion.1), channel_id=1, replica_groups=mesh['dp'=16,'mp'=2] {'mp'}, use_global_device_ids=true, to_apply=%region_3.0 | all-reduce | flops 512 | bytes 4096 | tf_op jit(solution)/shard_map/psum | solution.py:25
  396.2 0.0 copy-done
  396.2 16.0 %fusion.8 = bf16[512,14336]{0,1:T(8,128)(2,1)} fusion(bf16[16,512,896]{1,2,0:T(8,128)(2,1)} %copy.5, f32[512]{0:T(512)S(1)} %copy-done, f32[512]{0:T(512)S(1)} %multiply_add_fusion, f32[14336]{0:T(1024)S(1)} %sqrt.3), kind=kLoop, calls=%fused_computation.11 | loop fusion | flops 73400320 | bytes 29421568 | tf_op jit(solution)/shard_map/convert_element_type | solution.py:16
  412.2 19.9 %copy.6 = bf16[512,14336]{1,0:T(8,128)(2,1)} copy(bf16[512,14336]{0,1:T(8,128)(2,1)} %fusion.8) | data formatting | bytes 29360128 | tf_op jit(solution)/shard_map/convert_element_type | solution.py:16
  (3 shorter events, 0.0 us)
Async XLA Ops:
  0.0 363.7 %all-to-all-start = ((bf16[16,512,896]{2,1,0:T(8,128)(2,1)}), bf16[16,512,896]{2,1,0:T(8,128)(2,1)}, u32[]{:S(2)}, u32[]{:S(2)}) async-start(bf16[16,512,896]{2,1,0:T(8,128)(2,1)} %bitcast.22), calls=%async_computation | async-start | bytes 29360128 | tf_op jit(solution)/shard_map/all_to_all | solution.py:21
  384.4 11.9 %copy-start = (f32[512]{0:T(512)S(1)}, f32[512]{0:T(512)}, u32[]{:S(2)}) copy-start(f32[512]{0:T(512)} %param.5) | copy-start | bytes 6148
where the time goes:
time: 434 us; the launch traced here: 432 us
  blocking collectives  353 us (81%)
  local copies, waits for them, and re-layouts  40.6 us (9%)
  other arithmetic  31.4 us (7%)
  starting transfers between devices  7.46 us (2%)
    psum x1, blocking collectives, per_device(): squares = lax.psum(partial_value, 'dp')  348 us
    all_to_all x1, local copies, waits for them, and re-layouts, per_device(): lax.all_to_all(weight, 'dp', split_axis=0, concat_axis=1, tiled=True)  20.7 us
    convert_element_type x1, local copies, waits for them, and re-layouts, soft_prune(): return (wide * kept_share).astype(jnp.bfloat16)  19.9 us
    convert_element_type x1, other arithmetic, soft_prune(): return (wide * kept_share).astype(jnp.bfloat16)  16 us
  transfers between devices with their start and end apart: 1, of which 0 were waited for; matrix products, arithmetic and copies ran while one was open for 2% of the time, Pallas kernels for 0%

commit v1 on v0

--- a/solution.py
+++ b/solution.py
@@ -19,7 +19,8 @@
 def per_device(activations, weight, thresholds):
     partial_value = jnp.sum(jnp.square(activations.astype(jnp.float32)), axis=0)
     relaid = lax.all_to_all(weight, "dp", split_axis=0, concat_axis=1, tiled=True)
-    squares = lax.psum(partial_value, "dp")
+    parts = lax.all_gather(partial_value, "dp", axis=0, tiled=False)
+    squares = parts.sum(axis=0)
     col_norm = jnp.sqrt(squares)
     row_part = jnp.sum(jnp.abs(relaid.astype(jnp.float32)) * col_norm[None, :], axis=1)
     row_total = lax.psum(row_part, "mp")

time: 434 us -> 407 us (0.938)
  the two profiles are of different devices: /device:TPU:0 before, /device:TPU:10 now
where the time goes in v1:
time: 407 us; the launch traced here: 405 us
  blocking collectives  327 us (80%)
  local copies, waits for them, and re-layouts  40.8 us (10%)
  other arithmetic  31.6 us (8%)
  starting transfers between devices  6.3 us (2%)
    all_gather x1, blocking collectives, per_device(): parts = lax.all_gather(partial_value, 'dp', axis=0, tiled=False)  322 us
    all_to_all x1, local copies, waits for them, and re-layouts, per_device(): lax.all_to_all(weight, 'dp', split_axis=0, concat_axis=1, tiled=True)  20.7 us
    convert_element_type x1, local copies, waits for them, and re-layouts, soft_prune(): return (wide * kept_share).astype(jnp.bfloat16)  19.9 us
    convert_element_type x1, other arithmetic, soft_prune(): return (wide * kept_share).astype(jnp.bfloat16)  16 us
    reduce_sum x1, other arithmetic, per_device(): partial_value = jnp.sum(jnp.square(activations.astype(jnp.float32)), axis=0)  8.52 us
  transfers between devices with their start and end apart: 1, of which 0 were waited for; matrix products, arithmetic and copies ran while one was open for 2% of the time, Pallas kernels for 0%

profile of v1, /device:TPU:10, one launch (start us, length us, event | category | flops | bytes accessed | tf_op | source)
XLA Modules:
  0.0 405.4 jit_solution(17093228633388613221)
XLA Ops:
  0.0 6.3 %all-to-all-start = ((bf16[16,512,896]{2,1,0:T(8,128)(2,1)}), bf16[16,512,896]{2,1,0:T(8,128)(2,1)}, u32[]{:S(2)}, u32[]{:S(2)}) async-start(bf16[16,512,896]{2,1,0:T(8,128)(2,1)} %bitcast.22), calls=%async_computation | async-start | bytes 29360128 | tf_op jit(solution)/shard_map/all_to_all | solution.py:21
  6.3 8.5 %multiply_reduce_fusion = f32[14336]{0:T(1024)S(1)} fusion(bf16[512,14336]{1,0:T(8,128)(2,1)} %param.3), kind=kLoop, calls=%fused_computation.12 | loop fusion | flops 22005760 | bytes 14737408 | tf_op jit(solution)/shard_map/reduce_sum | solution.py:20
  14.8 321.9 %all-gather = f32[229376]{0:T(1024)S(1)} all-gather(f32[14336]{0:T(1024)S(1)} %multiply_reduce_fusion), channel_id=2, replica_groups=mesh['dp'=16,'mp'=2] {'dp'}, dimensions={0}, use_global_device_ids=true | all-gather | bytes 974848 | tf_op jit(solution)/shard_map/all_gather | solution.py:22
  336.7 0.1 reshape.20
  336.8 0.1 reduce_sum.28
  337.0 0.0 all-to-all-done
  337.0 20.7 %copy.7 = bf16[16,512,896]{1,2,0:T(8,128)(2,1)} copy(bf16[16,512,896]{2,1,0:T(8,128)(2,1)} %all-to-all-done) | data formatting | bytes 29360128 | tf_op jit(solution)/shard_map/all_to_all | solution.py:21
  357.7 0.0 copy-start
  357.7 6.9 %fusion.1 = f32[512]{0:T(512)S(1)} fusion(bf16[16,512,896]{1,2,0:T(8,128)(2,1)} %copy.7, f32[16,896]{1,0:T(8,128)S(1)} %sqrt.12), kind=kLoop, calls=%fused_computation.4 | loop fusion | flops 29359616 | bytes 14739456 | tf_op jit(solution)/shard_map/reduce_sum | solution.py:25
  364.6 4.9 %psum.7 = f32[512]{0:T(512)S(1)} all-reduce(f32[512]{0:T(512)S(1)} %fusion.1), channel_id=1, replica_groups=mesh['dp'=16,'mp'=2] {'mp'}, use_global_device_ids=true, to_apply=%region_3.0 | all-reduce | flops 512 | bytes 4096 | tf_op jit(solution)/shard_map/psum | solution.py:26
  369.6 0.0 copy-done
  369.6 16.0 %fusion.8 = bf16[512,14336]{0,1:T(8,128)(2,1)} fusion(bf16[16,512,896]{1,2,0:T(8,128)(2,1)} %copy.7, f32[512]{0:T(512)S(1)} %copy-done, f32[512]{0:T(512)S(1)} %multiply_add_fusion, f32[14336]{0:T(1024)S(1)} %sqrt.11), kind=kLoop, calls=%fused_computation.11 | loop fusion | flops 73400320 | bytes 29421568 | tf_op jit(solution)/shard_map/convert_element_type | solution.py:16
  385.5 19.9 %copy.8 = bf16[512,14336]{1,0:T(8,128)(2,1)} copy(bf16[512,14336]{0,1:T(8,128)(2,1)} %fusion.8) | data formatting | bytes 29360128 | tf_op jit(solution)/shard_map/convert_element_type | solution.py:16
  (3 shorter events, 0.0 us)
Async XLA Ops:
  0.0 337.0 %all-to-all-start = ((bf16[16,512,896]{2,1,0:T(8,128)(2,1)}), bf16[16,512,896]{2,1,0:T(8,128)(2,1)}, u32[]{:S(2)}, u32[]{:S(2)}) async-start(bf16[16,512,896]{2,1,0:T(8,128)(2,1)} %bitcast.22), calls=%async_computation | async-start | bytes 29360128 | tf_op jit(solution)/shard_map/all_to_all | solution.py:21
  357.7 11.9 %copy-start = (f32[512]{0:T(512)S(1)}, f32[512]{0:T(512)}, u32[]{:S(2)}) copy-start(f32[512]{0:T(512)} %param.5) | copy-start | bytes 6148
